TPU v7x, 32 devices: a whole 2x2x4 slice. The times are simulated.
32 devices in a mesh: dp: 2 (over y), fsdp: 16 (over z, x, core).
Axes of the slice: x: 2, y: 2, z: 4, core: 2. Of those that a mesh axis runs over, the one named last changes fastest.
Arguments:
- ids: int32 [2, 192], P('dp'), may hold values from 0 to 511
- embed: bfloat16 [512, 8192], P(None, 'fsdp'), may hold values from -32 to 32
- gain: bfloat16 [8192], P('fsdp'), may hold values from 0.099609375 to 1.8984375
- w_in: bfloat16 [3, 4096, 8192], P(None, 'fsdp'), may hold values from -0.0625 to 0.0625
- feat_filter: float32 [3, 256, 7], P(None, 'fsdp'), may hold values from -2.4 to 2.4
- inner_filter: float32 [256, 7], P('fsdp'), may hold values from -2.4 to 2.4
- w_out: bfloat16 [4096, 8192], P(None, 'fsdp'), may hold values from -0.09375 to 0.09375
- cotangent: bfloat16 [2, 192, 8192], P('dp', None, 'fsdp'), may hold values from -6 to 6
- right_prev: bfloat16 [8192, 256], P('fsdp'), may hold values from -6 to 6
Outputs:
- block_out: bfloat16 [2, 192, 8192], P('dp', None, 'fsdp')
- filter_grad: float32 [4, 256, 7], P(None, 'fsdp')
- basis: bfloat16 [4096, 256], P('fsdp')
- right_factor: float32 [8192, 256], P('fsdp')
All inputs are finite; a program needn't handle non-finite values.
Results may differ from a plain program's by a relative error of at most 0.014.
The roundings to bfloat16 on the way count: a program that leaves them out, or rounds other values in their place, can miss the bound.
Values may be sent and summed in bfloat16 or wider, within the bound.
No kernel may reach another device: no remote copies, remote signals or barrier semaphores. Data moves between devices by JAX's collectives and lax.ppermute only.
A program may use at most 128 MiB of HBM per device.

v0:
```python
import jax
import jax.numpy as jnp
from jax import lax
from jax.sharding import PartitionSpec as P

D = 8192
C = 4096
GROUP = 16


def shifted(signal, lag, tap_count):
    padded = jnp.pad(signal, ((tap_count - 1, 0), (0, 0)))
    first = tap_count - 1 - lag
    return padded[first : first + signal.shape[0]]


def causal(signal, tap_table):
    tap_count = tap_table.shape[0]
    result = jnp.zeros(signal.shape, jnp.float32)
    for lag in range(tap_count):
        result = result + tap_table[lag][None, :] * shifted(signal, lag, tap_count)
    return result


def anticausal(signal, tap_table):
    tap_count = tap_table.shape[0]
    padded = jnp.pad(signal, ((0, tap_count - 1), (0, 0)))
    result = jnp.zeros(signal.shape, jnp.float32)
    for lag in range(tap_count):
        result = result + tap_table[lag][None, :] * padded[lag : lag + signal.shape[0]]
    return result


def tap_sums(gradient, signal, tap_count):
    listing = []
    for lag in range(tap_count):
        listing.append(jnp.sum(gradient * shifted(signal, lag, tap_count), axis=0))
    stacked = jnp.stack(listing, axis=0)
    grouped = stacked.reshape(tap_count, stacked.shape[1] // GROUP, GROUP).sum(axis=2)
    return grouped.T


def expand(filters):
    return jnp.repeat(filters.T, GROUP, axis=1)


def per_device(ids, embed, gain, w_in, feat_filter, inner_filter, w_out, cotangent, right_prev):
    tokens = ids[0]
    length = tokens.shape[0]
    tap_count = inner_filter.shape[1]
    onehot = (tokens[:, None] == jnp.arange(embed.shape[0], dtype=jnp.int32)[None, :]).astype(
        jnp.bfloat16
    )
    x_cols = jnp.dot(onehot, embed, preferred_element_type=jnp.float32)
    square_sums = lax.psum(jnp.sum(x_cols * x_cols, axis=1), "fsdp")
    factor = lax.rsqrt(square_sums / D + 1e-05)
    normed_cols = (x_cols * factor[:, None] * gain.astype(jnp.float32)[None, :]).astype(
        jnp.bfloat16
    )
    projected = jnp.einsum(
        "ld,kcd->klc",
        lax.all_gather(normed_cols, "fsdp", axis=1, tiled=True),
        w_in,
        preferred_element_type=jnp.float32,
    )
    rounded = lax.optimization_barrier(projected.astype(jnp.bfloat16)).astype(jnp.float32)
    query, key_in, value = (rounded[0], rounded[1], rounded[2])
    query_conv = causal(query, expand(feat_filter[0]))
    key_conv = causal(key_in, expand(feat_filter[1]))
    value_conv = causal(value, expand(feat_filter[2]))
    gated = key_conv * value_conv
    inner_table = expand(inner_filter)
    window = causal(gated, inner_table)
    gated_out = (query_conv * window).astype(jnp.bfloat16)
    cot_cols = cotangent[0]
    shard_piece = lax.all_gather(gated_out, "fsdp", axis=1, tiled=True)
    weight_rows = w_out
    mixed_sum = jnp.dot(shard_piece, weight_rows, preferred_element_type=jnp.float32)
    term = jnp.einsum("lc,ld->cd", shard_piece, cot_cols, preferred_element_type=jnp.float32)
    mixed_sum, grad_part = (mixed_sum, term)
    block_out = (x_cols + mixed_sum).astype(jnp.bfloat16)[None]
    weight_rows = w_out
    mixed_grad = lax.psum_scatter(
        jnp.einsum("cd,ld->cl", weight_rows, cot_cols, preferred_element_type=jnp.float32),
        "fsdp",
        scatter_dimension=0,
        tiled=True,
    ).T
    query_grad = mixed_grad * window
    window_grad = mixed_grad * query_conv
    gated_grad = anticausal(window_grad, inner_table)
    key_grad = gated_grad * value_conv
    value_grad = gated_grad * key_conv
    norm_factor = 1.0 / jnp.sqrt(jnp.float32(lax.axis_size("dp") * length))
    filter_part = (
        jnp.stack(
            [
                tap_sums(query_grad, query, tap_count),
                tap_sums(key_grad, key_in, tap_count),
                tap_sums(value_grad, value, tap_count),
                tap_sums(window_grad, gated, tap_count),
            ],
            axis=0,
        )
        * norm_factor
    )
    grad_total, filter_grad = (
        lax.psum(grad_part.astype(jnp.bfloat16), "dp").astype(jnp.float32),
        lax.psum(filter_part.astype(jnp.bfloat16), "dp").astype(jnp.float32),
    )
    grad_half = grad_total.astype(jnp.bfloat16)
    grad_rows_own = lax.all_to_all(grad_half, "fsdp", split_axis=0, concat_axis=1, tiled=True)
    panel_own = jnp.dot(
        grad_rows_own,
        lax.all_gather(right_prev, "fsdp", axis=0, tiled=True),
        preferred_element_type=jnp.float32,
    ).astype(jnp.bfloat16)
    root_scale = jnp.sqrt(jnp.float32(C))
    gram_local = jnp.einsum("cr,cs->rs", panel_own, panel_own, preferred_element_type=jnp.float32)
    gram_matrix = lax.psum(gram_local, "fsdp")
    lower_factor = jnp.linalg.cholesky(gram_matrix)
    solved = jax.scipy.linalg.solve_triangular(
        lower_factor, panel_own.astype(jnp.float32).T, lower=True
    ).T
    basis_own = (solved * root_scale).astype(jnp.bfloat16)
    right_raw = jnp.einsum(
        "cd,cr->dr",
        grad_half,
        lax.all_gather(basis_own, "fsdp", axis=0, tiled=True),
        preferred_element_type=jnp.float32,
    )
    column_sums = lax.psum(jnp.sum(right_raw * right_raw, axis=0), "fsdp")
    right_factor = right_raw * lax.rsqrt(column_sums / D + 1e-06)[None, :]
    return (block_out, filter_grad, basis_own, right_factor)


def solution(mesh):
    placed = (
        P("dp", None),
        P(None, "fsdp"),
        P("fsdp"),
        P(None, "fsdp", None),
        P(None, "fsdp", None),
        P("fsdp", None),
        P(None, "fsdp"),
        P("dp", None, "fsdp"),
        P("fsdp", None),
    )
    return jax.shard_map(
        per_device,
        mesh=mesh,
        in_specs=placed,
        out_specs=(P("dp", None, "fsdp"), P(None, "fsdp", None), P("fsdp", None), P("fsdp", None)),
        check_vma=False,
    )
```

profile of v0, /device:TPU:0, one launch (start us, length us, event | category | flops | bytes accessed | tf_op | source)
XLA Modules:
  0.0 699.4 jit_solution(17935779332028869934)
XLA Ops:
  9.3 34.9 %psum.35 = f32[192]{0:T(256)S(1)} all-reduce(f32[192]{0:T(256)S(1)} %get-tuple-element.121), channel_id=1, replica_groups=mesh['dp'=2,'fsdp'=16] {'fsdp'}, use_global_device_ids=true, to_apply=%region_1.0 | all-reduce | flops 192 | bytes 1536 | tf_op jit(solution)/shard_map/psum | solution.py:55
  45.1 5.4 fusion.14
  55.0 34.7 %all-gather.5.cloned.1.call-done = bf16[192,8192]{1,0:T(8,128)(2,1)} async-done(((bf16[192,512]{1,0:T(8,128)(2,1)}), bf16[192,8192]{1,0:T(8,128)(2,1)}) %all-gather.5.cloned.1.call-update) | async-done | bytes 3145744 | tf_op jit(solution)/shard_map/all_gather | solution.py:62
  89.7 9.8 %fusion.6 = bf16[3,192,256]{2,1,0:T(8,128)(2,1)S(1)} fusion(bf16[3,256,8192]{2,1,0:T(8,128)(2,1)} %param.12, bf16[192,8192]{1,0:T(8,128)(2,1)} %all-gather.5.cloned.1.call-done), kind=kOutput, calls=%fused_computation.8 | convolution fusion | flops 2416066560 | bytes 16023552 | tf_op jit(solution)/shard_map/ld,kcd->klc/dot_general | solution.py:60
  99.6 58.3 %reduce-scatter.2.cloned.1.call-done = f32[256,192]{0,1:T(8,128)} async-done(((f32[4096,192]{0,1:T(8,128)}), f32[256,192]{0,1:T(8,128)}) %reduce-scatter.2.cloned.1.call-update) | async-done | bytes 196624 | tf_op jit(solution)/shard_map/reduce_scatter | solution.py:83
  164.3 38.0 %all-gather.7.cloned.1.call-done = bf16[192,4096]{1,0:T(8,128)(2,1)} async-done(((bf16[192,256]{1,0:T(8,128)(2,1)}), bf16[192,4096]{1,0:T(8,128)(2,1)}) %all-gather.7.cloned.1.call-update) | async-done | bytes 1572880 | tf_op jit(solution)/shard_map/all_gather | solution.py:76
  202.3 4.7 convolution_convert_fusion
  207.7 106.5 %all-reduce.9.cloned.1.call-done = bf16[4096,512]{1,0:T(8,128)(2,1)} async-done(((bf16[4096,512]{1,0:T(8,128)(2,1)}), bf16[4096,512]{1,0:T(8,128)(2,1)}) %all-reduce.9.cloned.1.call-update) | async-done | bytes 4194320 | tf_op jit(solution)/shard_map/psum | solution.py:108
  314.2 6.4 copy.22
  320.6 5.7 all-to-all-start
  326.3 94.7 %all-gather.9.cloned.1.call-done = bf16[8192,256]{1,0:T(8,128)(2,1)} async-done(((bf16[512,256]{1,0:T(8,128)(2,1)}), bf16[8192,256]{1,0:T(8,128)(2,1)}) %all-gather.9.cloned.1.call-update) | async-done | bytes 4194320 | tf_op jit(solution)/shard_map/all_gather | solution.py:115
  421.0 6.5 all-to-all-done
  427.4 4.8 convolution_convert_fusion.1
  434.0 103.0 %all-reduce.11.cloned.1.call-done = f32[256,256]{0,1:T(8,128)} async-done(((f32[256,256]{0,1:T(8,128)}), f32[256,256]{0,1:T(8,128)}) %all-reduce.11.cloned.1.call-update) | async-done | bytes 262160 | tf_op jit(solution)/shard_map/psum | solution.py:120
  540.6 11.7 %cholesky.50 = f32[128,128]{1,0:T(8,128)S(1)} custom-call(f32[128,128]{1,0:T(8,128)S(1)} %cholesky.118), custom_call_target="Cholesky" | custom-call | tf_op jit(solution)/shard_map/jit(cholesky)/cholesky | solution.py:121
  553.6 9.8 %custom-call.15 = f32[1,128,128]{1,2,0:T(8,128)S(1)} custom-call(f32[1,128,128]{2,1,0:T(8,128)S(1)} %get-tuple-element.89), custom_call_target="InvertDiagBlocksLowerTriangular" | custom-call | tf_op jit(solution)/shard_map/jit(cholesky)/cholesky | solution.py:121
  566.2 11.7 %cholesky.105 = f32[128,128]{1,0:T(8,128)S(1)} custom-call(f32[128,128]{1,0:T(8,128)S(1)} %convolution_subtract_fusion.1), custom_call_target="Cholesky" | custom-call | tf_op jit(solution)/shard_map/jit(cholesky)/cholesky | solution.py:121
  584.2 6.8 while.1
  591.0 20.5 %custom-call.16 = f32[2,128,128]{1,2,0:T(8,128)S(1)} custom-call(f32[2,128,128]{2,1,0:T(8,128)} %get-tuple-element.11), custom_call_target="InvertDiagBlocksLowerTriangular" | custom-call | tf_op jit(solution)/shard_map/jit(_solve_triangular)/triangular_solve | solution.py:122
  622.1 5.0 psum.36
  627.8 3.8 fusion.9
  632.4 23.5 %all-gather.11.cloned.1.call-done = bf16[4096,256]{0,1:T(8,128)(2,1)} async-done(((bf16[256,256]{0,1:T(8,128)(2,1)}), bf16[4096,256]{0,1:T(8,128)(2,1)}) %all-gather.11.cloned.1.call-update) | async-done | bytes 2097168 | tf_op jit(solution)/shard_map/all_gather | solution.py:129
  655.9 4.2 multiply_reduce_fusion
  660.1 31.6 %psum.39 = f32[256]{0:T(256)S(1)} all-reduce(f32[256]{0:T(256)S(1)} %get-tuple-element.125), channel_id=1, replica_groups=mesh['dp'=2,'fsdp'=16] {'fsdp'}, use_global_device_ids=true, to_apply=%region_43.44 | all-reduce | flops 256 | bytes 2048 | tf_op jit(solution)/shard_map/psum | solution.py:132
  (198 shorter events, 48.3 us)
Async XLA Ops:
  7.2 1.1 copy-start
  7.2 82.5 %all-gather.5.cloned.1.call-start = ((), (), s32[]{:S(2)}) async-start(), calls=%async_computation.2 | async-start | bytes 3342336 | tf_op jit(solution)/shard_map/all_gather | solution.py:62
  45.0 5.5 copy-start.8
  45.0 6.6 copy-start.9
  45.1 112.9 %reduce-scatter.2.cloned.1.call-start = ((), (), s32[]{:S(2)}) async-start(), calls=%async_computation.4 | async-start | bytes 3342336 | tf_op jit(solution)/shard_map/reduce_scatter | solution.py:83
  50.5 151.8 %all-gather.7.cloned.1.call-start = ((), (), s32[]{:S(2)}) async-start(), calls=%async_computation.3 | async-start | bytes 1671168 | tf_op jit(solution)/shard_map/all_gather | solution.py:76
  99.5 102.8 %copy-start.7 = (bf16[1,192,512]{2,1,0:T(8,128)(2,1)S(1)}, bf16[1,192,512]{2,1,0:T(8,128)(2,1)}, u32[]{:S(2)}) copy-start(bf16[1,192,512]{2,1,0:T(8,128)(2,1)} %param.16) | copy-start | bytes 589828
  99.6 61.3 %copy-start.3 = (f32[192,256]{1,0:T(8,128)}, f32[192,256]{1,0:T(8,128)S(1)}, u32[]{:S(2)}) copy-start(f32[192,256]{1,0:T(8,128)S(1)} %get-tuple-element.84) | copy-start | bytes 589828
  159.1 48.0 %copy-start.4 = (f32[192,256]{1,0:T(8,128)}, f32[192,256]{1,0:T(8,128)S(1)}, u32[]{:S(2)}) copy-start(f32[192,256]{1,0:T(8,128)S(1)} %get-tuple-element.79) | copy-start | bytes 589828
  161.0 46.1 %copy-start.2 = (f32[192,256]{1,0:T(8,128)}, f32[192,256]{1,0:T(8,128)S(1)}, u32[]{:S(2)}) copy-start(f32[192,256]{1,0:T(8,128)S(1)} %mul.459) | copy-start | bytes 589828
  164.2 150.0 %all-reduce.9.cloned.1.call-start = ((), (), s32[]{:S(2)}) async-start(), calls=%async_computation.5 | async-start | bytes 8388608 | tf_op jit(solution)/shard_map/psum | solution.py:108
  207.1 213.9 %all-gather.9.cloned.1.call-start = ((), (), s32[]{:S(2)}) async-start(), calls=%async_computation.6 | async-start | bytes 4456448 | tf_op jit(solution)/shard_map/all_gather | solution.py:115
  320.6 106.8 %all-to-all-start = ((bf16[16,256,512]{1,2,0:T(8,128)(2,1)}), bf16[16,256,512]{1,2,0:T(8,128)(2,1)}, u32[]{:S(2)}, u32[]{:S(2)}) async-start(bf16[16,256,512]{1,2,0:T(8,128)(2,1)} %copy.22), calls=%async_computation.1 | async-start | bytes 8388608 | tf_op jit(solution)/shard_map/all_to_all | solution.py:112
  326.2 210.8 %all-reduce.11.cloned.1.call-start = ((), (), s32[]{:S(2)}) async-start(), calls=%async_computation.7 | async-start | bytes 524288 | tf_op jit(solution)/shard_map/psum | solution.py:120
  433.2 222.7 %all-gather.11.cloned.1.call-start = ((), (), s32[]{:S(2)}) async-start(), calls=%async_computation.8 | async-start | bytes 2228224 | tf_op jit(solution)/shard_map/all_gather | solution.py:129
  434.0 193.8 %copy-start.1 = (bf16[192,4096]{1,0:T(8,128)(2,1)S(1)}, bf16[192,4096]{1,0:T(8,128)(2,1)}, u32[]{:S(2)}) copy-start(bf16[192,4096]{1,0:T(8,128)(2,1)} %all-gather.7.cloned.1.call-done) | copy-start | bytes 4718596
  539.9 0.7 copy-start.6
  616.6 15.0 %copy-start.5 = (bf16[256,256]{0,1:T(8,128)(2,1)S(1)}, bf16[256,256]{0,1:T(8,128)(2,1)}, u32[]{:S(2)}) copy-start(bf16[256,256]{0,1:T(8,128)(2,1)} %fusion.19) | copy-start | bytes 393220
Sparse Core Ops, SparseCore 0:
  45.2 44.4 all-gather.4
  93.5 64.4 reduce-scatter.1
  164.4 37.9 all-gather.6
  207.2 106.9 all-reduce.8
  316.4 104.4 all-gather.8
  433.3 103.7 all-reduce.10
  614.1 41.7 all-gather.10
where the time goes:
time: 700 us; the launch traced here: 699 us
  waiting for transfers between devices  466 us (67%)
  other arithmetic  73.8 us (11%)
  blocking collectives  71.5 us (10%)
  matrix products  39.3 us (6%)
  local copies, waits for them, and re-layouts  26.9 us (4%)
  between operations  15.8 us (2%)
    psum x1, waiting for transfers between devices, per_device(): lax.psum(grad_part.astype(jnp.bfloat16), 'dp').astype(jnp.float32)  107 us
    psum x1, waiting for transfers between devices, per_device(): gram_matrix = lax.psum(gram_local, 'fsdp')  103 us
    all_gather x1, waiting for transfers between devices, per_device(): lax.all_gather(right_prev, 'fsdp', axis=0, tiled=True)  94.7 us
    reduce_scatter x1, waiting for transfers between devices, per_device(): lax.psum_scatter(jnp.einsum('cd,ld->cl', weight_rows, cot_cols, preferred...  58.3 us
    all_gather x1, waiting for transfers between devices, per_device(): shard_piece = lax.all_gather(gated_out, 'fsdp', axis=1, tiled=True)  38 us
    another operation x7, other arithmetic, per_device(): lower_factor = jnp.linalg.cholesky(gram_matrix)  36.4 us
    psum x1, blocking collectives, per_device(): square_sums = lax.psum(jnp.sum(x_cols * x_cols, axis=1), 'fsdp')  34.9 us
    all_gather x1, waiting for transfers between devices, per_device(): lax.all_gather(normed_cols, 'fsdp', axis=1, tiled=True)  34.7 us
  transfers between devices with their start and end apart: 8, of which 8 were waited for; matrix products, arithmetic and copies ran while one was open for 6% of the time, Pallas kernels for 0%

commit v1 on v0

--- a/solution.py
+++ b/solution.py
@@ -73,7 +73,22 @@
     window = causal(gated, inner_table)
     gated_out = (query_conv * window).astype(jnp.bfloat16)
     cot_cols = cotangent[0]
-    shard_piece = lax.all_gather(gated_out, "fsdp", axis=1, tiled=True)
+
+    def prepare_sites(sheet, dimension_no=1):
+        p_count = lax.axis_size("fsdp")
+        made = [(tick, (tick + 1) % p_count) for tick in range(p_count)]
+
+        def choose_seats_all(big):
+            if len(big) == p_count:
+                return big
+            return choose_seats_all([lax.ppermute(big[0], axis_name="fsdp", perm=made), *big])
+
+        f_now = jnp.concatenate(choose_seats_all([sheet]), dimension_no)
+        return jnp.roll(
+            f_now, (lax.axis_index("fsdp") + 1) * sheet.shape[dimension_no], dimension_no
+        )
+
+    shard_piece = prepare_sites(gated_out)
     weight_rows = w_out
     mixed_sum = jnp.dot(shard_piece, weight_rows, preferred_element_type=jnp.float32)
     term = jnp.einsum("lc,ld->cd", shard_piece, cot_cols, preferred_element_type=jnp.float32)

time: 700 us -> 760 us (1.086)
  waiting for transfers between devices: 466 us -> 530 us
  other arithmetic: 73.8 us -> 64.6 us
  local copies, waits for them, and re-layouts: 26.9 us -> 35.2 us
    ppermute x0 -> x15, waiting for transfers between devices: none -> 101 us  [choose_seats_all(): lax.ppermute(big[0], axis_name='fsdp', perm=made)]
    all_gather x1 -> x0, waiting for transfers between devices: 38 us -> none  [per_device(): shard_piece = lax.all_gather(gated_out, 'fsdp', axis=1, tiled=True)]
    unnamed x46 -> x95, local copies, waits for them, and re-layouts: 2.47 us -> 15.9 us
  transfers between devices with their start and end apart: 8 -> 22, of which waited for: 8 -> 22; matrix products, arithmetic and copies ran while one was open for 6% -> 5% of each run, Pallas kernels for 0% -> 0%
where the time goes in v1:
time: 760 us; the launch traced here: 759 us
  waiting for transfers between devices  530 us (70%)
  blocking collectives  71.5 us (9%)
  other arithmetic  64.6 us (8%)
  matrix products  35.3 us (5%)
  local copies, waits for them, and re-layouts  35.2 us (5%)
  between operations  16.1 us (2%)
    psum x1, waiting for transfers between devices, per_device(): lax.psum(grad_part.astype(jnp.bfloat16), 'dp').astype(jnp.float32)  105 us
    psum x1, waiting for transfers between devices, per_device(): gram_matrix = lax.psum(gram_local, 'fsdp')  104 us
    ppermute x15, waiting for transfers between devices, choose_seats_all(): lax.ppermute(big[0], axis_name='fsdp', perm=made)  101 us
    all_gather x1, waiting for transfers between devices, per_device(): lax.all_gather(right_prev, 'fsdp', axis=0, tiled=True)  94.5 us
    reduce_scatter x1, waiting for transfers between devices, per_device(): lax.psum_scatter(jnp.einsum('cd,ld->cl', weight_rows, cot_cols, preferred...  58.4 us
    psum x1, blocking collectives, per_device(): square_sums = lax.psum(jnp.sum(x_cols * x_cols, axis=1), 'fsdp')  34.9 us
    another operation x7, other arithmetic, per_device(): lower_factor = jnp.linalg.cholesky(gram_matrix)  34.6 us
    all_gather x1, waiting for transfers between devices, per_device(): lax.all_gather(normed_cols, 'fsdp', axis=1, tiled=True)  34.1 us
  transfers between devices with their start and end apart: 22, of which 22 were waited for; matrix products, arithmetic and copies ran while one was open for 5% of the time, Pallas kernels for 0%

profile of v1, /device:TPU:0, one launch (start us, length us, event | category | flops | bytes accessed | tf_op | source)
XLA Modules:
  0.0 759.4 jit_solution(17949368555458908828)
XLA Ops:
  9.3 34.9 %psum.35 = f32[192]{0:T(256)S(1)} all-reduce(f32[192]{0:T(256)S(1)} %get-tuple-element.121), channel_id=1, replica_groups=mesh['dp'=2,'fsdp'=16] {'fsdp'}, use_global_device_ids=true, to_apply=%region_1.0 | all-reduce | flops 192 | bytes 1536 | tf_op jit(solution)/shard_map/psum | solution.py:55
  55.6 34.1 %all-gather.4.cloned.1.call-done = bf16[192,8192]{1,0:T(8,128)(2,1)} async-done(((bf16[192,512]{1,0:T(8,128)(2,1)}), bf16[192,8192]{1,0:T(8,128)(2,1)}) %all-gather.4.cloned.1.call-update) | async-done | bytes 3145744 | tf_op jit(solution)/shard_map/all_gather | solution.py:62
  89.7 9.8 %fusion.14 = bf16[3,192,256]{2,1,0:T(8,128)(2,1)S(1)} fusion(bf16[3,256,8192]{2,1,0:T(8,128)(2,1)} %param.12, bf16[192,8192]{1,0:T(8,128)(2,1)} %all-gather.4.cloned.1.call-done), kind=kOutput, calls=%fused_computation.11 | convolution fusion | flops 2416066560 | bytes 16023552 | tf_op jit(solution)/shard_map/ld,kcd->klc/dot_general | solution.py:60
  99.6 58.4 %reduce-scatter.2.cloned.1.call-done = f32[256,192]{0,1:T(8,128)} async-done(((f32[4096,192]{0,1:T(8,128)}), f32[256,192]{0,1:T(8,128)}) %reduce-scatter.2.cloned.1.call-update) | async-done | bytes 196624 | tf_op jit(solution)/shard_map/reduce_scatter | solution.py:98
  168.2 6.7 collective-permute-done.1
  181.7 6.7 collective-permute-done.3
  188.4 6.7 collective-permute-done.4
  201.9 6.7 collective-permute-done.6
  208.6 6.7 collective-permute-done.7
  215.4 6.7 collective-permute-done.8
  222.1 6.7 collective-permute-done.9
  229.5 6.7 collective-permute-done.10
  236.9 6.7 collective-permute-done.11
  251.6 6.8 collective-permute-done.13
  258.6 7.0 collective-permute-done.14
  280.6 104.7 %all-reduce.9.cloned.1.call-done = bf16[4096,512]{1,0:T(8,128)(2,1)} async-done(((bf16[4096,512]{1,0:T(8,128)(2,1)}), bf16[4096,512]{1,0:T(8,128)(2,1)}) %all-reduce.9.cloned.1.call-update) | async-done | bytes 4194320 | tf_op jit(solution)/shard_map/psum | solution.py:123
  397.5 94.5 %all-gather.6.cloned.1.call-done = bf16[8192,256]{1,0:T(8,128)(2,1)} async-done(((bf16[512,256]{1,0:T(8,128)(2,1)}), bf16[8192,256]{1,0:T(8,128)(2,1)}) %all-gather.6.cloned.1.call-update) | async-done | bytes 4194320 | tf_op jit(solution)/shard_map/all_gather | solution.py:130
  504.3 103.7 %all-reduce.11.cloned.1.call-done = f32[256,256]{0,1:T(8,128)} async-done(((f32[256,256]{0,1:T(8,128)}), f32[256,256]{0,1:T(8,128)}) %all-reduce.11.cloned.1.call-update) | async-done | bytes 262160 | tf_op jit(solution)/shard_map/psum | solution.py:135
  610.1 11.7 %cholesky.50 = f32[128,128]{1,0:T(8,128)S(1)} custom-call(f32[128,128]{1,0:T(8,128)S(1)} %cholesky.118), custom_call_target="Cholesky" | custom-call | tf_op jit(solution)/shard_map/jit(cholesky)/cholesky | solution.py:136
  621.9 9.8 %custom-call.15 = f32[1,128,128]{1,2,0:T(8,128)S(1)} custom-call(f32[1,128,128]{2,1,0:T(8,128)S(1)} %get-tuple-element.89), custom_call_target="InvertDiagBlocksLowerTriangular" | custom-call | tf_op jit(solution)/shard_map/jit(cholesky)/cholesky | solution.py:136
  632.2 11.7 %cholesky.105 = f32[128,128]{1,0:T(8,128)S(1)} custom-call(f32[128,128]{1,0:T(8,128)S(1)} %convolution_subtract_fusion.1), custom_call_target="Cholesky" | custom-call | tf_op jit(solution)/shard_map/jit(cholesky)/cholesky | solution.py:136
  651.9 20.5 %custom-call.16 = f32[2,128,128]{1,2,0:T(8,128)S(1)} custom-call(f32[2,128,128]{2,1,0:T(8,128)} %get-tuple-element.11), custom_call_target="InvertDiagBlocksLowerTriangular" | custom-call | tf_op jit(solution)/shard_map/jit(_solve_triangular)/triangular_solve | solution.py:137
  689.3 26.6 %all-gather.8.cloned.1.call-done = bf16[4096,256]{0,1:T(8,128)(2,1)} async-done(((bf16[256,256]{0,1:T(8,128)(2,1)}), bf16[4096,256]{0,1:T(8,128)(2,1)}) %all-gather.8.cloned.1.call-update) | async-done | bytes 2097168 | tf_op jit(solution)/shard_map/all_gather | solution.py:144
  720.1 31.6 %psum.39 = f32[256]{0:T(256)S(1)} all-reduce(f32[256]{0:T(256)S(1)} %get-tuple-element.125), channel_id=1, replica_groups=mesh['dp'=2,'fsdp'=16] {'fsdp'}, use_global_device_ids=true, to_apply=%region_43.44 | all-reduce | flops 256 | bytes 2048 | tf_op jit(solution)/shard_map/psum | solution.py:147
  (275 shorter events, 122.1 us)
Async XLA Ops:
  7.2 82.5 %all-gather.4.cloned.1.call-start = ((), (), s32[]{:S(2)}) async-start(), calls=%async_computation.2 | async-start | bytes 3342336 | tf_op jit(solution)/shard_map/all_gather | solution.py:62
  45.0 112.9 %reduce-scatter.2.cloned.1.call-start = ((), (), s32[]{:S(2)}) async-start(), calls=%async_computation.3 | async-start | bytes 3342336 | tf_op jit(solution)/shard_map/reduce_scatter | solution.py:98
  50.5 334.7 %all-reduce.9.cloned.1.call-start = ((), (), s32[]{:S(2)}) async-start(), calls=%async_computation.4 | async-start | bytes 8388608 | tf_op jit(solution)/shard_map/psum | solution.py:123
  161.4 6.8 collective-permute-start
  168.2 6.7 collective-permute-start.1
  174.9 6.7 collective-permute-start.2
  181.7 6.7 collective-permute-start.3
  188.4 6.7 collective-permute-start.4
  195.1 6.7 collective-permute-start.5
  201.9 6.7 collective-permute-start.6
  208.6 6.7 collective-permute-start.7
  215.4 43.1 %copy-start.5 = (bf16[192,256]{1,0:T(8,128)(2,1)}, bf16[192,256]{1,0:T(8,128)(2,1)S(1)}, u32[]{:S(2)}) copy-start(bf16[192,256]{1,0:T(8,128)(2,1)S(1)} %collective-permute-done.7) | copy-start | bytes 294916
  215.4 6.7 collective-permute-start.8
  222.1 36.4 %copy-start.7 = (bf16[192,256]{1,0:T(8,128)(2,1)}, bf16[192,256]{1,0:T(8,128)(2,1)S(1)}, u32[]{:S(2)}) copy-start(bf16[192,256]{1,0:T(8,128)(2,1)S(1)} %collective-permute-done.8) | copy-start | bytes 294916
  222.1 6.7 collective-permute-start.9
  229.5 6.7 collective-permute-start.10
  236.9 6.7 collective-permute-start.11
  244.2 6.7 collective-permute-start.12
  251.6 6.8 collective-permute-start.13
  258.5 7.1 collective-permute-start.14
  280.0 212.0 %all-gather.6.cloned.1.call-start = ((), (), s32[]{:S(2)}) async-start(), calls=%async_computation.5 | async-start | bytes 4456448 | tf_op jit(solution)/shard_map/all_gather | solution.py:130
  391.6 106.9 %all-to-all-start = ((bf16[16,256,512]{1,2,0:T(8,128)(2,1)}), bf16[16,256,512]{1,2,0:T(8,128)(2,1)}, u32[]{:S(2)}, u32[]{:S(2)}) async-start(bf16[16,256,512]{1,2,0:T(8,128)(2,1)} %copy.22), calls=%async_computation.1 | async-start | bytes 8388608 | tf_op jit(solution)/shard_map/all_to_all | solution.py:127
  397.3 210.7 %all-reduce.11.cloned.1.call-start = ((), (), s32[]{:S(2)}) async-start(), calls=%async_computation.6 | async-start | bytes 524288 | tf_op jit(solution)/shard_map/psum | solution.py:135
  504.2 211.7 %all-gather.8.cloned.1.call-start = ((), (), s32[]{:S(2)}) async-start(), calls=%async_computation.7 | async-start | bytes 2228224 | tf_op jit(solution)/shard_map/all_gather | solution.py:144
  (17 other events, 130.1 us)
Sparse Core Ops, SparseCore 0:
  45.2 44.4 all-gather.3
  93.5 64.4 reduce-scatter.1
  280.1 105.0 all-reduce.8
  387.5 104.4 all-gather.5
  504.3 103.6 all-reduce.10
  674.2 41.6 all-gather.7
